TPU v7x, 1024 devices: a whole 4x8x16 slice. The times are simulated.
1024 devices in a mesh: dp: 4 (over y_hi), blk: 32 (over y_lo, z), head: 8 (over x, core).
Axes of the slice: x: 4, y: 8 (y_hi: 4, y_lo: 2; y = y_hi * 2 + y_lo), z: 16, core: 2. Of those that a mesh axis runs over, the one named last changes fastest.
Arguments:
- queries: bfloat16 [65536, 2048], P(('dp', 'blk', 'head')), parts along dimension 0, may hold values from -5 to 5
- key_states: bfloat16 [65536, 2048], P(('dp', 'blk', 'head')), parts along dimension 0, may hold values from -5 to 5
- value_states: bfloat16 [65536, 2048], P(('dp', 'blk', 'head')), parts along dimension 0, may hold values from -6 to 6
- upstream: bfloat16 [65536, 2048], P(('dp', 'blk'), 'head'), parts along dimension 0, may hold values from -6 to 6
- clip_lengths: int32 [128], P('dp'), parts along dimension 0, may hold values from 1 to 1024, 16384 in all
Outputs:
- attended: bfloat16 [65536, 2048], P(('dp', 'blk'), 'head'), parts along dimension 0
- query_grads: bfloat16 [65536, 2048], P(('dp', 'blk'), 'head'), parts along dimension 0
- key_grads: bfloat16 [65536, 2048], P(('dp', 'blk'), 'head'), parts along dimension 0
- value_grads: bfloat16 [65536, 2048], P(('dp', 'blk'), 'head'), parts along dimension 0
There are 4 independent parts, one for each index of `dp`. A program takes and returns all parts, laid end to end along the dimension named above; each array names one. Nothing has to cross between parts.
Inputs may be any that keep to these rules, and one draw needn't show every extreme that they name: `clip_lengths`: 32 clip lengths that sum to 16384; the longest has exactly 1024 tokens.
All inputs are finite; a program needn't handle non-finite values.
Results may differ from a plain program's by a relative error of at most 0.015.
Values may be sent and summed in bfloat16 or wider, within the bound.
A program may use at most 32 MiB of HBM per device.

v0:
```python
import jax
import jax.numpy as jnp
from jax import lax
from jax.sharding import PartitionSpec as P

HEAD_DIM = 128


masked_fill = -1e30


def shifted(block, axis, distance):
    devices = range(lax.axis_size(axis))
    route = [(i - distance, i) for i in devices if i - distance in devices]
    return lax.ppermute(block, axis, route)


def clip_index(clip_ends, positions, seq_total):
    counted = jnp.sum((positions[:, None] >= clip_ends[None, :]).astype(jnp.int32), axis=1)
    inside = (positions >= 0) & (positions < seq_total)
    return jnp.where(inside, counted, -1)


def head_columns(rows, head_index):
    return rows[:, head_index * HEAD_DIM : (head_index + 1) * HEAD_DIM]


def head_window(query_head, key_head, value_head, upstream_head, same_clip):
    score_scale = HEAD_DIM ** (-0.5)
    scores = score_scale * jnp.einsum(
        "qe,ke->qk", query_head, key_head, preferred_element_type=jnp.float32
    )
    scores = jnp.where(same_clip, scores, masked_fill)
    row_max = jnp.max(scores, axis=1, keepdims=True)
    totals = jnp.sum(jnp.where(same_clip, jnp.exp(scores - row_max), 0.0), axis=1, keepdims=True)
    log_norm = row_max + jnp.log(totals)
    chances = jnp.where(same_clip, jnp.exp(scores - log_norm), 0.0)
    weights = chances.astype(jnp.bfloat16)
    attended = jnp.dot(weights, value_head, preferred_element_type=jnp.float32).astype(jnp.bfloat16)
    offsets = jnp.sum(upstream_head.astype(jnp.float32) * attended.astype(jnp.float32), axis=1)
    dchances = jnp.einsum(
        "qe,ke->qk", upstream_head, value_head, preferred_element_type=jnp.float32
    )
    dscores = (chances * (dchances - offsets[:, None])).astype(jnp.bfloat16)
    query_part = score_scale * jnp.dot(dscores, key_head, preferred_element_type=jnp.float32)
    key_part = score_scale * jnp.einsum(
        "qk,qe->ke", dscores, query_head, preferred_element_type=jnp.float32
    )
    value_part = jnp.einsum("qk,qe->ke", weights, upstream_head, preferred_element_type=jnp.float32)
    return (attended, query_part, key_part, value_part, log_norm[:, 0], offsets)


def window_pass(query_rows, key_window, value_window, upstream, same_clip):
    heads_here = query_rows.shape[1] // HEAD_DIM
    collected = [[], [], [], [], [], []]
    for head_index in range(heads_here):
        outcome = head_window(
            head_columns(query_rows, head_index),
            head_columns(key_window, head_index),
            head_columns(value_window, head_index),
            head_columns(upstream, head_index),
            same_clip,
        )
        for field_index in range(6):
            collected[field_index].append(outcome[field_index])
    attended = jnp.concatenate(collected[0], axis=1)
    query_part = jnp.concatenate(collected[1], axis=1)
    key_part = jnp.concatenate(collected[2], axis=1)
    value_part = jnp.concatenate(collected[3], axis=1)
    return (
        attended,
        query_part,
        key_part,
        value_part,
        jnp.stack(collected[4]),
        jnp.stack(collected[5]),
    )


def pass_keys(key_rows, value_rows):
    return shifted(jnp.stack([key_rows, value_rows]), "blk", 1)


def on_device(queries, key_states, value_states, upstream, clip_lengths):
    query_rows, key_rows, value_rows = (
        lax.all_to_all(queries, "head", split_axis=1, concat_axis=0, tiled=True),
        lax.all_to_all(key_states, "head", split_axis=1, concat_axis=0, tiled=True),
        lax.all_to_all(value_states, "head", split_axis=1, concat_axis=0, tiled=True),
    )
    previous = pass_keys(key_rows, value_rows)
    block_rows = upstream.shape[0]
    clip_ends = jnp.cumsum(clip_lengths)
    seq_total = block_rows * lax.axis_size("blk")
    first_row = lax.axis_index("blk") * block_rows
    positions = first_row - block_rows + jnp.arange(3 * block_rows, dtype=jnp.int32)
    all_ids = clip_index(clip_ends, positions, seq_total)
    window_ids = all_ids[: 2 * block_rows]
    own_ids = all_ids[block_rows : 2 * block_rows]
    window_mask = own_ids[:, None] == window_ids[None, :]
    key_window = jnp.concatenate([previous[0], key_rows], axis=0)
    value_window = jnp.concatenate([previous[1], value_rows], axis=0)
    attended, query_part, key_part, value_part, log_norm, offsets = window_pass(
        query_rows, key_window, value_window, upstream, window_mask
    )
    returned = shifted(jnp.stack([key_part[:block_rows], value_part[:block_rows]]), "blk", -1)
    key_total = key_part[block_rows:] + returned[0]
    value_total = value_part[block_rows:] + returned[1]
    return (
        attended,
        query_part.astype(jnp.bfloat16),
        key_total.astype(jnp.bfloat16),
        value_total.astype(jnp.bfloat16),
    )


def solution(mesh):
    return jax.shard_map(
        on_device,
        mesh=mesh,
        in_specs=(
            P(("dp", "blk", "head"), None),
            P(("dp", "blk", "head"), None),
            P(("dp", "blk", "head"), None),
            P(("dp", "blk"), "head"),
            P("dp"),
        ),
        out_specs=(
            P(("dp", "blk"), "head"),
            P(("dp", "blk"), "head"),
            P(("dp", "blk"), "head"),
            P(("dp", "blk"), "head"),
        ),
        check_vma=False,
    )
```

profile of v0, /device:TPU:57, one launch (start us, length us, event | category | flops | bytes accessed | tf_op | source)
XLA Modules:
  0.0 96.4 jit_solution(4491582199629236504)
XLA Ops:
  0.6 0.0 copy-start.4
  0.6 0.0 copy-start.1
  0.7 0.0 copy-start
  0.7 1.7 %copy.65 = bf16[8,8,8,256]{3,2,0,1:T(8,128)(2,1)} copy(bf16[8,8,8,256]{3,2,1,0:T(8,128)(2,1)} %bitcast.78) | data formatting | bytes 524288 | tf_op jit(solution)/shard_map/all_to_all | solution.py:87
  2.4 5.0 %all-to-all-start = ((bf16[64,8,256]{2,0,1:T(8,128)(2,1)}), bf16[64,8,256]{2,0,1:T(8,128)(2,1)S(1)}, u32[]{:S(2)}, u32[]{:S(2)}) async-start(bf16[64,8,256]{2,0,1:T(8,128)(2,1)} %bitcast.63), calls=%async_computation | async-start | bytes 524288 | tf_op jit(solution)/shard_map/all_to_all | solution.py:87
  7.4 1.7 %copy.64 = bf16[8,8,8,256]{3,2,0,1:T(8,128)(2,1)} copy(bf16[8,8,8,256]{3,2,1,0:T(8,128)(2,1)} %bitcast.79) | data formatting | bytes 524288 | tf_op jit(solution)/shard_map/all_to_all | solution.py:88
  9.0 4.8 %all-to-all-done = bf16[64,8,256]{2,0,1:T(8,128)(2,1)S(1)} async-done(((bf16[64,8,256]{2,0,1:T(8,128)(2,1)}), bf16[64,8,256]{2,0,1:T(8,128)(2,1)S(1)}, u32[]{:S(2)}, u32[]{:S(2)}) %all-to-all-start) | async-done | bytes 262176 | tf_op jit(solution)/shard_map/all_to_all | solution.py:87
  13.8 4.4 %all-to-all-start.1 = ((bf16[64,8,256]{2,0,1:T(8,128)(2,1)}), bf16[64,8,256]{2,0,1:T(8,128)(2,1)S(1)}, u32[]{:S(2)}, u32[]{:S(2)}) async-start(bf16[64,8,256]{2,0,1:T(8,128)(2,1)} %bitcast.62), calls=%async_computation.1 | async-start | bytes 524288 | tf_op jit(solution)/shard_map/all_to_all | solution.py:88
  18.2 0.0 copy-done.4
  18.2 0.1 copy.45
  18.3 0.1 reduce-window.8
  18.3 0.1 reduce
  18.4 0.0 copy-done.1
  18.5 0.7 copy.63
  19.2 5.5 %all-to-all-done.1 = bf16[64,8,256]{2,0,1:T(8,128)(2,1)S(1)} async-done(((bf16[64,8,256]{2,0,1:T(8,128)(2,1)}), bf16[64,8,256]{2,0,1:T(8,128)(2,1)S(1)}, u32[]{:S(2)}, u32[]{:S(2)}) %all-to-all-start.1) | async-done | bytes 262176 | tf_op jit(solution)/shard_map/all_to_all | solution.py:88
  24.7 4.4 %all-to-all-start.2 = ((bf16[64,8,256]{2,0,1:T(8,128)(2,1)}), bf16[64,8,256]{2,0,1:T(8,128)(2,1)S(1)}, u32[]{:S(2)}, u32[]{:S(2)}) async-start(bf16[64,8,256]{2,0,1:T(8,128)(2,1)} %bitcast.61), calls=%async_computation.2 | async-start | bytes 524288 | tf_op jit(solution)/shard_map/all_to_all | solution.py:86
  29.0 0.1 pad_maximum_fusion.3
  29.1 4.0 %collective-permute-start = (bf16[2,512,256]{2,1,0:T(8,128)(2,1)S(1)}, bf16[2,512,256]{2,1,0:T(8,128)(2,1)S(1)}, u32[]{:S(2)}, u32[]{:S(2)}) collective-permute-start(bf16[2,512,256]{2,1,0:T(8,128)(2,1)S(1)} %pad_maximum_fusion.3), channel_id=1, source_target_pairs={{0,8},{8,16},{16,24},{24,32},{32,40},{40,48},{48,56},{56,64},{64,7... | collective-permute-start | bytes 1572872 | tf_op jit(solution)/shard_map/ppermute | solution.py:15
  33.1 0.1 convert_reduce_fusion
  33.2 0.0 copy-done
  33.3 0.1 copy.55
  33.4 0.1 copy.56
  33.5 26.5 %collective-permute-done = bf16[2,512,256]{2,1,0:T(8,128)(2,1)S(1)} collective-permute-done((bf16[2,512,256]{2,1,0:T(8,128)(2,1)S(1)}, bf16[2,512,256]{2,1,0:T(8,128)(2,1)S(1)}, u32[]{:S(2)}, u32[]{:S(2)}) %collective-permute-start) | collective-permute-done | bytes 524320 | tf_op jit(solution)/shard_map/ppermute | solution.py:15
  60.0 0.0 copy-start.2
  60.0 0.0 all-to-all-done.2
  60.1 0.5 fusion.38
  60.5 0.5 fusion.37
  61.0 0.0 copy-done.2
  61.0 0.8 fusion
  61.8 0.7 fusion.4
  62.5 0.5 fusion.29
  63.0 1.0 %multiply_reduce_fusion.1 = (f32[512]{0:T(512)S(1)}, bf16[512,128]{0,1:T(8,128)(2,1)}) fusion(bf16[512,128]{0,1:T(8,128)(2,1)S(1)} %copy.55, bf16[512,1024]{0,1:T(8,128)(2,1)S(1)} %get-tuple-element.32, bf16[512,256]{1,0:T(8,128)(2,1)S(1)} %get-tuple-element.28, bf16[512,256]{1,0:T(8,128)(2,1)S(1)} %bitcast.65), kind=kOutput, calls=%fused_computation.56 | convolution fusion | flops 135069184 | bytes 1837056 | tf_op jit(solution)/shard_map/dot_general | solution.py:39
  64.0 0.6 fusion.3
  64.6 0.5 fusion.26
  65.1 0.4 multiply_reduce_fusion
  65.5 0.6 fusion.2
  66.2 0.5 convolution_multiply_fusion
  66.6 0.5 convolution_multiply_fusion.1
  67.2 0.0 copy-start.3
  67.2 0.1 pad_maximum_fusion
  67.3 3.1 %collective-permute-start.1 = (f32[2,512,256]{1,2,0:T(8,128)S(1)}, f32[2,512,256]{1,2,0:T(8,128)}, u32[]{:S(2)}, u32[]{:S(2)}) collective-permute-start(f32[2,512,256]{1,2,0:T(8,128)S(1)} %pad_maximum_fusion), channel_id=1, source_target_pairs={{8,0},{16,8},{24,16},{32,24},{40,32},{48,40},{56,48},{64,56},{72,6... | collective-permute-start | bytes 3145736 | tf_op jit(solution)/shard_map/ppermute | solution.py:15
  70.4 0.0 copy-done.3
  70.4 0.4 fusion.7
  70.8 0.3 fusion.6
  71.2 0.8 copy.52
  72.0 0.9 pad_maximum_fusion.6
  72.9 0.8 copy.51
  73.8 19.6 %collective-permute-done.1 = f32[2,512,256]{1,2,0:T(8,128)} collective-permute-done((f32[2,512,256]{1,2,0:T(8,128)S(1)}, f32[2,512,256]{1,2,0:T(8,128)}, u32[]{:S(2)}, u32[]{:S(2)}) %collective-permute-start.1) | collective-permute-done | bytes 1048608 | tf_op jit(solution)/shard_map/ppermute | solution.py:15
  93.3 1.4 %fusion.14 = (bf16[512,256]{0,1:T(8,128)(2,1)S(1)}, bf16[512,256]{0,1:T(8,128)(2,1)S(1)}) fusion(f32[2,512,256]{1,2,0:T(8,128)} %collective-permute-done.1, f32[1024,128]{0,1:T(8,128)S(1)} %fusion.26, f32[1024,128]{0,1:T(8,128)S(1)} %fusion.29, f32[1024,128]{0,1:T(8,128)S(1)} %convolution_multiply_fusion, f32[1024,128]{0,1:T(8,128)S(1)} %convolution_multiply_fusion.1), kind=kLoop, calls=%fused_computation.34 | loop fusion | flops 786432 | bytes 3670016 | tf_op jit(solution)/shard_map/convert_element_type | solution.py:112
  94.7 0.8 copy.54
  95.5 0.8 copy.53
  (10 shorter events, 0.2 us)
Async XLA Ops:
  0.6 17.6 %copy-start.4 = (s32[32]{0:T(128)S(1)}, s32[32]{0:T(128)}, u32[]{:S(2)}) copy-start(s32[32]{0:T(128)} %param.9) | copy-start | bytes 388
  0.6 17.8 %copy-start.1 = (bf16[64,2048]{1,0:T(8,128)(2,1)S(1)}, bf16[64,2048]{1,0:T(8,128)(2,1)}, u32[]{:S(2)}) copy-start(bf16[64,2048]{1,0:T(8,128)(2,1)} %param.5) | copy-start | bytes 786436
  0.7 32.6 %copy-start = (bf16[512,256]{1,0:T(8,128)(2,1)S(1)}, bf16[512,256]{1,0:T(8,128)(2,1)}, u32[]{:S(2)}) copy-start(bf16[512,256]{1,0:T(8,128)(2,1)} %param.8) | copy-start | bytes 786436
  2.4 11.4 %all-to-all-start = ((bf16[64,8,256]{2,0,1:T(8,128)(2,1)}), bf16[64,8,256]{2,0,1:T(8,128)(2,1)S(1)}, u32[]{:S(2)}, u32[]{:S(2)}) async-start(bf16[64,8,256]{2,0,1:T(8,128)(2,1)} %bitcast.63), calls=%async_computation | async-start | bytes 524288 | tf_op jit(solution)/shard_map/all_to_all | solution.py:87
  13.8 10.9 %all-to-all-start.1 = ((bf16[64,8,256]{2,0,1:T(8,128)(2,1)}), bf16[64,8,256]{2,0,1:T(8,128)(2,1)S(1)}, u32[]{:S(2)}, u32[]{:S(2)}) async-start(bf16[64,8,256]{2,0,1:T(8,128)(2,1)} %bitcast.62), calls=%async_computation.1 | async-start | bytes 524288 | tf_op jit(solution)/shard_map/all_to_all | solution.py:88
  24.7 35.4 %all-to-all-start.2 = ((bf16[64,8,256]{2,0,1:T(8,128)(2,1)}), bf16[64,8,256]{2,0,1:T(8,128)(2,1)S(1)}, u32[]{:S(2)}, u32[]{:S(2)}) async-start(bf16[64,8,256]{2,0,1:T(8,128)(2,1)} %bitcast.61), calls=%async_computation.2 | async-start | bytes 524288 | tf_op jit(solution)/shard_map/all_to_all | solution.py:86
  29.1 30.9 %collective-permute-start = (bf16[2,512,256]{2,1,0:T(8,128)(2,1)S(1)}, bf16[2,512,256]{2,1,0:T(8,128)(2,1)S(1)}, u32[]{:S(2)}, u32[]{:S(2)}) collective-permute-start(bf16[2,512,256]{2,1,0:T(8,128)(2,1)S(1)} %pad_maximum_fusion.3), channel_id=1, source_target_pairs={{0,8},{8,16},{16,24},{24,32},{32,40},{40,48},{48,56},{56,64},{64,7... | collective-permute-start | bytes 1572872 | tf_op jit(solution)/shard_map/ppermute | solution.py:15
  60.0 1.0 copy-start.2
  67.2 3.2 %copy-start.3 = (bf16[512,256]{1,0:T(8,128)(2,1)S(1)}, bf16[512,256]{1,0:T(8,128)(2,1)}, u32[]{:S(2)}) copy-start(bf16[512,256]{1,0:T(8,128)(2,1)} %copy-done.2) | copy-start | bytes 786436
  67.3 26.0 %collective-permute-start.1 = (f32[2,512,256]{1,2,0:T(8,128)S(1)}, f32[2,512,256]{1,2,0:T(8,128)}, u32[]{:S(2)}, u32[]{:S(2)}) collective-permute-start(f32[2,512,256]{1,2,0:T(8,128)S(1)} %pad_maximum_fusion), channel_id=1, source_target_pairs={{8,0},{16,8},{24,16},{32,24},{40,32},{48,40},{56,48},{64,56},{72,6... | collective-permute-start | bytes 3145736 | tf_op jit(solution)/shard_map/ppermute | solution.py:15
where the time goes:
time: 97.8 us; the launch traced here: 96.4 us
  waiting for transfers between devices  56.3 us (58%)
  starting transfers between devices  20.8 us (21%)
  local copies, waits for them, and re-layouts  7.88 us (8%)
  matrix products  6.19 us (6%)
  other arithmetic  4.29 us (4%)
    ppermute x2, waiting for transfers between devices, shifted(): return lax.ppermute(block, axis, route)  46 us
    ppermute x2, starting transfers between devices, shifted(): return lax.ppermute(block, axis, route)  7.1 us
    all_to_all x1, waiting for transfers between devices, on_device(): lax.all_to_all(value_states, 'head', split_axis=1, concat_axis=0, tiled=T...  5.5 us
    all_to_all x1, starting transfers between devices, on_device(): lax.all_to_all(key_states, 'head', split_axis=1, concat_axis=0, tiled=True)  4.97 us
    all_to_all x1, waiting for transfers between devices, on_device(): lax.all_to_all(key_states, 'head', split_axis=1, concat_axis=0, tiled=True)  4.8 us
    all_to_all x1, starting transfers between devices, on_device(): lax.all_to_all(value_states, 'head', split_axis=1, concat_axis=0, tiled=T...  4.36 us
    all_to_all x1, starting transfers between devices, on_device(): lax.all_to_all(queries, 'head', split_axis=1, concat_axis=0, tiled=True)  4.36 us
    unnamed x17, local copies, waits for them, and re-layouts  3.64 us
  transfers between devices with their start and end apart: 5, of which 4 were waited for; matrix products, arithmetic and copies ran while one was open for 7% of the time, Pallas kernels for 0%

commit v1 on v0

v1 whole, which is shorter than its diff:
```python
import functools

import jax
import jax.numpy as jnp
from jax import lax
from jax.experimental import pallas as pl
from jax.experimental.pallas import tpu as pltpu
from jax.sharding import PartitionSpec as P

HEAD_DIM = 128
SCALE = HEAD_DIM ** (-0.5)
LOG2E = 1.4426950408889634
MESH = pl.DeviceIdType.MESH
MASKED = -1e30
K, V, Q, U = 0, 1, 2, 3
PARTNERS = ((0, 1), (1, 0), (3, 0), (1, 1), (3, 1), (2, 0), (2, 1))

NT = (((1,), (1,)), ((), ()))
TN = (((0,), (0,)), ((), ()))


def dot(a, b, dims=(((1,), (0,)), ((), ()))):
    return lax.dot_general(a, b, dims, preferred_element_type=jnp.float32)


def kernel(
    heads_here, blocks, chunk,
    q_hbm, k_hbm, v_hbm, u_hbm, lengths,
    att_ref, dq_ref, dk_ref, dv_ref,
    ks, vs, qs, us, kid, qid, stat_out, stat_in, dk_acc, dv_acc,
    own_sem, sx, rx, sz, rz, ss, rs,
):
    part, blk, me = lax.axis_index("dp"), lax.axis_index("blk"), lax.axis_index("head")
    group = lax.axis_size("head")
    rows = q_hbm.shape[0]
    block = rows * group
    wide = heads_here * HEAD_DIM
    chip, core = me // 2, lax.rem(me, 2)
    chips = group // 2
    after, before = lax.rem(blk + 1, blocks), lax.rem(blk + blocks - 1, blocks)

    def to(dx, dc):
        return lax.rem(chip + dx, chips) * 2 + lax.rem(core + dc, 2)

    def source(dx, dc):
        return lax.rem(chip + chips - dx, chips) * 2 + lax.rem(core + dc, 2)

    barrier = pltpu.get_barrier_semaphore()
    for dx, dc in PARTNERS:
        pl.semaphore_signal(barrier, inc=1, device_id=(part, blk, to(dx, dc)), device_id_type=MESH)
    for other in (after, before):
        pl.semaphore_signal(barrier, inc=1, device_id=(part, other, me), device_id_type=MESH)
    pl.semaphore_wait(barrier, len(PARTNERS) + 2)

    inputs = (k_hbm, v_hbm, q_hbm)
    held = (ks, vs, qs)

    def columns(owner, h):
        return pl.ds(pl.multiple_of(owner * wide + h * HEAD_DIM, HEAD_DIM), HEAD_DIM)

    def place(owner, second):
        return pl.ds(pl.multiple_of(owner * rows + second * block, rows), rows)

    def own_half(a):
        return 1 if a in (K, V) else 0

    def neighbour(a):
        return (part, after, me) if a in (K, V) else (part, before, me)

    def x_copy(a, h, dx, dc, owner, target):
        return pltpu.make_async_remote_copy(
            src_ref=inputs[a].at[:, columns(target, h)],
            dst_ref=held[a].at[h, place(owner, own_half(a)), :],
            send_sem=sx.at[a, h],
            recv_sem=rx.at[a, h, dx * 2 + dc],
            device_id=(part, blk, target),
            device_id_type=MESH,
        )

    def z_copy(a, h, owner, src):
        return pltpu.make_async_remote_copy(
            src_ref=src,
            dst_ref=held[a].at[h, place(owner, 1 - own_half(a)), :],
            send_sem=sz.at[a, h],
            recv_sem=rz.at[a, h],
            device_id=neighbour(a),
            device_id_type=MESH,
        )

    def z_all(a, h):
        ref = us if a == U else held[a]
        half = 0 if a in (K, V) else 1
        whole = ref.at[h, half * block : (half + 1) * block, :]
        return pltpu.make_async_remote_copy(
            src_ref=whole, dst_ref=whole, send_sem=sz.at[a, h], recv_sem=rz.at[a, h],
            device_id=neighbour(a), device_id_type=MESH,
        )

    def x_sent(a, h):
        part_of = held[a].at[h, 0 : len(PARTNERS) * rows, :]
        return pltpu.make_async_remote_copy(
            src_ref=part_of, dst_ref=part_of, send_sem=sx.at[a, h], recv_sem=rx.at[a, h, 0],
            device_id=(part, blk, to(0, 1)), device_id_type=MESH,
        )

    own = []
    for h in range(heads_here):
        for a in (K, V, Q):
            for dx, dc in PARTNERS:
                x_copy(a, h, dx, dc, me, to(dx, dc)).start()
            z_copy(a, h, me, inputs[a].at[:, columns(me, h)]).start()
        pltpu.make_async_remote_copy(
            src_ref=u_hbm.at[:, h * HEAD_DIM : (h + 1) * HEAD_DIM],
            dst_ref=us.at[h, block : 2 * block, :],
            send_sem=sz.at[U, h],
            recv_sem=rz.at[U, h],
            device_id=neighbour(U),
            device_id_type=MESH,
        ).start()
        for a in (K, V, Q):
            own.append(pltpu.make_async_copy(
                inputs[a].at[:, columns(me, h)],
                held[a].at[h, place(me, own_half(a)), :], own_sem.at[a, h]))
        own.append(pltpu.make_async_copy(
            u_hbm.at[:, h * HEAD_DIM : (h + 1) * HEAD_DIM], us.at[h, 0:block, :], own_sem.at[U, h]))
    for copy in own:
        copy.start()

    spread = 3 * block
    positions = (blk - 1) * block + lax.broadcasted_iota(jnp.int32, (1, spread), 1)
    counted = jnp.zeros((1, spread), jnp.int32)
    end = jnp.int32(0)
    for c in range(lengths.shape[0]):
        end = end + lengths[c]
        counted = counted + jnp.where(positions >= end, 1, 0)
    inside = (positions >= 0) & (positions < blocks * block)
    ids = jnp.where(inside, counted, -1)
    qid[...] = jnp.broadcast_to(ids[:, block:], qid.shape)
    for c in range(2 * block // HEAD_DIM):
        one = jnp.broadcast_to(ids[:, c * HEAD_DIM : (c + 1) * HEAD_DIM], (HEAD_DIM, HEAD_DIM))
        turned = one.T
        for n in range(chunk // HEAD_DIM):
            kid[c * HEAD_DIM : (c + 1) * HEAD_DIM, n * HEAD_DIM : (n + 1) * HEAD_DIM] = turned

    for h in range(heads_here):
        for a in (K, V, Q):
            for dx, dc in PARTNERS:
                owner = source(dx, dc)
                x_copy(a, h, dx, dc, owner, me).wait_recv()
                z_copy(a, h, owner, held[a].at[h, place(owner, own_half(a)), :]).start()
    for copy in own:
        copy.wait()

    def main(h):
        for a in (K, V):
            z_all(a, h).wait_recv()
        side = slice(h * HEAD_DIM, (h + 1) * HEAD_DIM)
        dk_acc[h] = jnp.zeros_like(dk_acc[h])
        dv_acc[h] = jnp.zeros_like(dv_acc[h])

        def step(c, carry):
            at = pl.ds(pl.multiple_of(c * chunk, chunk), chunk)
            query, up = qs[h, at, :], us[h, at, :]
            key, value = ks[h], vs[h]
            same = kid[...] == qid[0:1, at]
            scores = jnp.where(same, dot(key, query, NT), MASKED)
            top = jnp.max(scores, axis=0, keepdims=True)
            powers = jnp.exp2((scores - top) * (SCALE * LOG2E))
            total = jnp.sum(powers, axis=0, keepdims=True)
            chances = powers * (1.0 / total)
            weights = chances.astype(jnp.bfloat16)
            attended = dot(value, weights, TN).T.astype(jnp.bfloat16)
            att_ref[at, side] = attended
            products = up.astype(jnp.float32) * attended.astype(jnp.float32)
            offsets = jnp.sum(products.T, axis=0, keepdims=True)
            stat_out[h, 0:1, at] = top * (SCALE * LOG2E) + jnp.log2(total)
            stat_out[h, 1:2, at] = offsets
            dscores = (chances * (dot(value, up, NT) - offsets)).astype(jnp.bfloat16)
            dq_ref[at, side] = (dot(key, dscores, TN) * SCALE).T.astype(jnp.bfloat16)
            dv_acc[h] += dot(weights[block:], up)
            dk_acc[h] += dot(dscores[block:], query)
            return carry

        lax.fori_loop(0, block // chunk, step, 0)

    def stat_copy(h):
        return pltpu.make_async_remote_copy(
            src_ref=stat_out.at[h], dst_ref=stat_in.at[h], send_sem=ss.at[h], recv_sem=rs.at[h],
            device_id=(part, before, me), device_id_type=MESH,
        )

    def cross(h):
        z_all(Q, h).wait_recv()
        z_all(U, h).wait_recv()
        stat_copy(h).wait_recv()
        side = slice(h * HEAD_DIM, (h + 1) * HEAD_DIM)

        def step(c, carry):
            at = pl.ds(pl.multiple_of(c * chunk, chunk), chunk)
            there = pl.ds(pl.multiple_of(c * chunk + block, chunk), chunk)
            query, up = qs[h, there, :], us[h, there, :]
            key, value = ks[h, block:, :], vs[h, block:, :]
            same = kid[block:, :] == qid[0:1, there]
            powers = jnp.exp2(dot(key, query, NT) * (SCALE * LOG2E) - stat_in[h, 0:1, at])
            chances = jnp.where(same, powers, 0.0)
            dscores = chances * (dot(value, up, NT) - stat_in[h, 1:2, at])
            dv_acc[h] += dot(chances.astype(jnp.bfloat16), up)
            dk_acc[h] += dot(dscores.astype(jnp.bfloat16), query)
            return carry

        lax.fori_loop(0, block // chunk, step, 0)
        dk_ref[:, side] = (dk_acc[h] * SCALE).astype(jnp.bfloat16)
        dv_ref[:, side] = dv_acc[h].astype(jnp.bfloat16)

    for h in range(heads_here):
        main(h)
        stat_copy(h).start()
    for h in range(heads_here):
        cross(h)

    for h in range(heads_here):
        stat_copy(h).wait_send()
        for a in (K, V, Q):
            x_sent(a, h).wait_send()
        for a in (K, V, Q, U):
            z_all(a, h).wait_send()


def on_device(queries, key_states, value_states, upstream, clip_lengths):
    block, wide = upstream.shape
    heads_here = wide // HEAD_DIM
    chunk = 256
    group = lax.axis_size("head")
    blocks = lax.axis_size("blk")
    hbm = pl.BlockSpec(memory_space=pl.ANY)
    vmem = pl.BlockSpec(memory_space=pltpu.VMEM)
    out = jax.ShapeDtypeStruct((block, wide), jnp.bfloat16)
    return pl.pallas_call(
        functools.partial(kernel, heads_here, blocks, chunk),
        out_shape=(out,) * 4,
        in_specs=[hbm] * 4 + [pl.BlockSpec(memory_space=pltpu.SMEM)],
        out_specs=(vmem,) * 4,
        scratch_shapes=[
            pltpu.VMEM((heads_here, 2 * block, HEAD_DIM), jnp.bfloat16),
            pltpu.VMEM((heads_here, 2 * block, HEAD_DIM), jnp.bfloat16),
            pltpu.VMEM((heads_here, 2 * block, HEAD_DIM), jnp.bfloat16),
            pltpu.VMEM((heads_here, 2 * block, HEAD_DIM), jnp.bfloat16),
            pltpu.VMEM((2 * block, chunk), jnp.int32),
            pltpu.VMEM((8, 2 * block), jnp.int32),
            pltpu.VMEM((heads_here, 8, block), jnp.float32),
            pltpu.VMEM((heads_here, 8, block), jnp.float32),
            pltpu.VMEM((heads_here, block, HEAD_DIM), jnp.float32),
            pltpu.VMEM((heads_here, block, HEAD_DIM), jnp.float32),
            pltpu.SemaphoreType.DMA((4, heads_here)),
            pltpu.SemaphoreType.DMA((3, heads_here)),
            pltpu.SemaphoreType.DMA((3, heads_here, group)),
            pltpu.SemaphoreType.DMA((4, heads_here)),
            pltpu.SemaphoreType.DMA((4, heads_here)),
            pltpu.SemaphoreType.DMA((heads_here,)),
            pltpu.SemaphoreType.DMA((heads_here,)),
        ],
        compiler_params=pltpu.CompilerParams(collective_id=0, has_side_effects=True),
    )(queries, key_states, value_states, upstream, clip_lengths)


def solution(mesh):
    return jax.shard_map(
        on_device,
        mesh=mesh,
        in_specs=(
            P(("dp", "blk", "head"), None),
            P(("dp", "blk", "head"), None),
            P(("dp", "blk", "head"), None),
            P(("dp", "blk"), "head"),
            P("dp"),
        ),
        out_specs=(P(("dp", "blk"), "head"),) * 4,
        check_vma=False,
    )
```

time: 97.8 us -> 49.6 us (0.51)
  the two profiles are of different devices: /device:TPU:57 before, /device:TPU:16 now
where the time goes in v1:
time: 49.6 us; the launch traced here: 49.4 us
  Pallas kernels  44.2 us (89%)
  local copies, waits for them, and re-layouts  4.5 us (9%)
  between operations  0.65 us (1%)
    pallas_call x1, Pallas kernels, on_device(): pl.pallas_call(functools.partial(kernel, heads_here, blocks, chunk), out_...  44.2 us
    unnamed x10, local copies, waits for them, and re-layouts  4.5 us

profile of v1, /device:TPU:16, one launch (start us, length us, event | category | flops | bytes accessed | tf_op | source)
XLA Modules:
  0.0 49.4 jit_solution(16019886342203501362)
XLA Ops:
  0.6 44.2 %shard_map.84 = (bf16[512,256]{1,0:T(8,128)(2,1)}, bf16[512,256]{1,0:T(8,128)(2,1)}, bf16[512,256]{1,0:T(8,128)(2,1)}, bf16[512,256]{1,0:T(8,128)(2,1)}) custom-call(bf16[64,2048]{1,0:T(8,128)(2,1)} %q_hbm.1, bf16[64,2048]{1,0:T(8,128)(2,1)} %k_hbm.1, bf16[64,2048]{1,0:T(8,128)(2,1)} %v_hbm.1, bf16[512,256]{1,0:T(8,128)(2,1)} %u_hbm.1, s32[32]{0:T(128)} %lengths.1), custom_call_target="tpu_custom_call" | custom-call | tf_op jit(solution)/shard_map/pallas_call | solution.py:238
  44.9 0.0 copy-start.2
  44.9 1.7 %copy.13 = bf16[512,256]{1,0:T(8,128)(2,1)} copy(bf16[512,256]{1,0:T(8,128)(2,1)} %get-tuple-element.8) | data formatting | bytes 524288
  46.6 0.0 copy-done.2
  46.6 0.0 copy-start.1
  46.6 0.7 %copy.14 = bf16[512,256]{1,0:T(8,128)(2,1)} copy(bf16[512,256]{1,0:T(8,128)(2,1)S(1)} %copy-done.2) | data formatting | bytes 524288
  47.3 0.3 copy-done.1
  47.6 0.0 copy-start
  47.6 0.7 %copy.15 = bf16[512,256]{1,0:T(8,128)(2,1)} copy(bf16[512,256]{1,0:T(8,128)(2,1)S(1)} %copy-done.1) | data formatting | bytes 524288
  48.3 0.3 copy-done
  48.7 0.7 %copy.16 = bf16[512,256]{1,0:T(8,128)(2,1)} copy(bf16[512,256]{1,0:T(8,128)(2,1)S(1)} %copy-done) | data formatting | bytes 524288
Async XLA Ops:
  44.9 1.7 %copy-start.2 = (bf16[512,256]{1,0:T(8,128)(2,1)S(1)}, bf16[512,256]{1,0:T(8,128)(2,1)}, u32[]{:S(2)}) copy-start(bf16[512,256]{1,0:T(8,128)(2,1)} %get-tuple-element.9) | copy-start | bytes 786436
  46.6 1.0 %copy-start.1 = (bf16[512,256]{1,0:T(8,128)(2,1)S(1)}, bf16[512,256]{1,0:T(8,128)(2,1)}, u32[]{:S(2)}) copy-start(bf16[512,256]{1,0:T(8,128)(2,1)} %get-tuple-element.10) | copy-start | bytes 786436
  47.6 1.0 %copy-start = (bf16[512,256]{1,0:T(8,128)(2,1)S(1)}, bf16[512,256]{1,0:T(8,128)(2,1)}, u32[]{:S(2)}) copy-start(bf16[512,256]{1,0:T(8,128)(2,1)} %get-tuple-element.11) | copy-start | bytes 786436

commit v2 on v1

--- a/solution.py
+++ b/solution.py
@@ -28,7 +28,7 @@
     q_hbm, k_hbm, v_hbm, u_hbm, lengths,
     att_ref, dq_ref, dk_ref, dv_ref,
     ks, vs, qs, us, kid, qid, stat_out, stat_in, dk_acc, dv_acc,
-    own_sem, sx, rx, sz, rz, ss, rs,
+    own_sem, sx, rx, sz, rz, ss, rs, ready, odds,
 ):
     part, blk, me = lax.axis_index("dp"), lax.axis_index("blk"), lax.axis_index("head")
     group = lax.axis_size("head")
@@ -45,13 +45,6 @@
     def source(dx, dc):
         return lax.rem(chip + chips - dx, chips) * 2 + lax.rem(core + dc, 2)
 
-    barrier = pltpu.get_barrier_semaphore()
-    for dx, dc in PARTNERS:
-        pl.semaphore_signal(barrier, inc=1, device_id=(part, blk, to(dx, dc)), device_id_type=MESH)
-    for other in (after, before):
-        pl.semaphore_signal(barrier, inc=1, device_id=(part, other, me), device_id_type=MESH)
-    pl.semaphore_wait(barrier, len(PARTNERS) + 2)
-
     inputs = (k_hbm, v_hbm, q_hbm)
     held = (ks, vs, qs)
 
@@ -106,23 +99,19 @@
     own = []
     for h in range(heads_here):
         for a in (K, V, Q):
-            for dx, dc in PARTNERS:
-                x_copy(a, h, dx, dc, me, to(dx, dc)).start()
-            z_copy(a, h, me, inputs[a].at[:, columns(me, h)]).start()
-        pltpu.make_async_remote_copy(
-            src_ref=u_hbm.at[:, h * HEAD_DIM : (h + 1) * HEAD_DIM],
-            dst_ref=us.at[h, block : 2 * block, :],
-            send_sem=sz.at[U, h],
-            recv_sem=rz.at[U, h],
-            device_id=neighbour(U),
-            device_id_type=MESH,
-        ).start()
-        for a in (K, V, Q):
             own.append(pltpu.make_async_copy(
                 inputs[a].at[:, columns(me, h)],
                 held[a].at[h, place(me, own_half(a)), :], own_sem.at[a, h]))
         own.append(pltpu.make_async_copy(
             u_hbm.at[:, h * HEAD_DIM : (h + 1) * HEAD_DIM], us.at[h, 0:block, :], own_sem.at[U, h]))
+    barrier = pltpu.get_barrier_semaphore()
+    for dx, dc in PARTNERS:
+        pl.semaphore_signal(barrier, inc=1, device_id=(part, blk, to(dx, dc)), device_id_type=MESH)
+
+    @pl.when(blk > 0)
+    def _():
+        pl.semaphore_signal(barrier, inc=1, device_id=(part, before, me), device_id_type=MESH)
+
     for copy in own:
         copy.start()
 
@@ -142,46 +131,137 @@
         for n in range(chunk // HEAD_DIM):
             kid[c * HEAD_DIM : (c + 1) * HEAD_DIM, n * HEAD_DIM : (n + 1) * HEAD_DIM] = turned
 
+    @pl.when(blk == 0)
+    def _():
+        for h in range(heads_here):
+            ks[h, 0:block, :] = jnp.zeros((block, HEAD_DIM), jnp.bfloat16)
+            vs[h, 0:block, :] = jnp.zeros((block, HEAD_DIM), jnp.bfloat16)
+
+    pl.semaphore_wait(barrier, len(PARTNERS) + 1 - blk // (blocks - 1))
+
+    has_after, has_before = blk < blocks - 1, blk > 0
+    late_before = blk == blocks // 2
+
+    @pl.when(has_after)
+    def _():
+        pl.semaphore_signal(ready, inc=1, device_id=(part, after, me), device_id_type=MESH)
+
+    def back_up(h):
+        pltpu.make_async_remote_copy(
+            src_ref=u_hbm.at[:, h * HEAD_DIM : (h + 1) * HEAD_DIM],
+            dst_ref=us.at[h, block : 2 * block, :],
+            send_sem=sz.at[U, h],
+            recv_sem=rz.at[U, h],
+            device_id=neighbour(U),
+            device_id_type=MESH,
+        ).start()
+
+    def own_on(a, h):
+        z_copy(a, h, me, inputs[a].at[:, columns(me, h)]).start()
+
+    def on(a, h, owner):
+        z_copy(a, h, owner, held[a].at[h, place(owner, own_half(a)), :]).start()
+
+    for h in range(heads_here):
+        for a in (K, V):
+            for dx, dc in PARTNERS:
+                x_copy(a, h, dx, dc, me, to(dx, dc)).start()
+
+            @pl.when(has_after)
+            def _():
+                own_on(a, h)
+
+        for dx, dc in PARTNERS:
+            x_copy(Q, h, dx, dc, me, to(dx, dc)).start()
+
+    early_back = has_before & jnp.logical_not(late_before)
+
+    @pl.when(early_back)
+    def _():
+        pl.semaphore_wait(ready, 1)
+        for h in range(heads_here):
+            back_up(h)
+            own_on(Q, h)
+
     for h in range(heads_here):
         for a in (K, V, Q):
             for dx, dc in PARTNERS:
                 owner = source(dx, dc)
                 x_copy(a, h, dx, dc, owner, me).wait_recv()
-                z_copy(a, h, owner, held[a].at[h, place(owner, own_half(a)), :]).start()
+
+                @pl.when(early_back if a == Q else has_after)
+                def _():
+                    on(a, h, owner)
+
+    @pl.when(late_before)
+    def _():
+        pl.semaphore_wait(ready, 1)
+        for h in range(heads_here):
+            back_up(h)
+            own_on(Q, h)
+            for dx, dc in PARTNERS:
+                on(Q, h, source(dx, dc))
+
     for copy in own:
         copy.wait()
 
-    def main(h):
-        for a in (K, V):
-            z_all(a, h).wait_recv()
+    steps = block // chunk
+
+    def chunk_at(c):
+        return pl.ds(pl.multiple_of(c * chunk, chunk), chunk)
+
+    def scores_of(h):
+        @pl.when(has_before)
+        def _():
+            z_all(K, h).wait_recv()
+
+        def step(c, carry):
+            at = chunk_at(c)
+            same = kid[...] == qid[0:1, at]
+            scores = jnp.where(same, dot(ks[h], qs[h, at, :], NT), MASKED)
+            top = jnp.max(scores, axis=0, keepdims=True)
+            powers = jnp.exp2((scores - top) * (SCALE * LOG2E))
+            total = jnp.sum(powers, axis=0, keepdims=True)
+            odds[:, at] = powers * (1.0 / total)
+            stat_out[h, 0:1, at] = top * (SCALE * LOG2E) + jnp.log2(total)
+            return carry
+
+        lax.fori_loop(0, steps, step, 0)
+
+    def output_of(h):
+        @pl.when(has_before)
+        def _():
+            z_all(V, h).wait_recv()
+
+        side = slice(h * HEAD_DIM, (h + 1) * HEAD_DIM)
+
+        def step(c, carry):
+            at = chunk_at(c)
+            weights = odds[:, at].astype(jnp.bfloat16)
+            attended = dot(vs[h], weights, TN).T.astype(jnp.bfloat16)
+            att_ref[at, side] = attended
+            products = us[h, at, :].astype(jnp.float32) * attended.astype(jnp.float32)
+            stat_out[h, 1:2, at] = jnp.sum(products.T, axis=0, keepdims=True)
+            return carry
+
+        lax.fori_loop(0, steps, step, 0)
+
+    def grads_of(h):
         side = slice(h * HEAD_DIM, (h + 1) * HEAD_DIM)
         dk_acc[h] = jnp.zeros_like(dk_acc[h])
         dv_acc[h] = jnp.zeros_like(dv_acc[h])
 
         def step(c, carry):
-            at = pl.ds(pl.multiple_of(c * chunk, chunk), chunk)
+            at = chunk_at(c)
             query, up = qs[h, at, :], us[h, at, :]
-            key, value = ks[h], vs[h]
-            same = kid[...] == qid[0:1, at]
-            scores = jnp.where(same, dot(key, query, NT), MASKED)
-            top = jnp.max(scores, axis=0, keepdims=True)
-            powers = jnp.exp2((scores - top) * (SCALE * LOG2E))
-            total = jnp.sum(powers, axis=0, keepdims=True)
-            chances = powers * (1.0 / total)
-            weights = chances.astype(jnp.bfloat16)
-            attended = dot(value, weights, TN).T.astype(jnp.bfloat16)
-            att_ref[at, side] = attended
-            products = up.astype(jnp.float32) * attended.astype(jnp.float32)
-            offsets = jnp.sum(products.T, axis=0, keepdims=True)
-            stat_out[h, 0:1, at] = top * (SCALE * LOG2E) + jnp.log2(total)
-            stat_out[h, 1:2, at] = offsets
-            dscores = (chances * (dot(value, up, NT) - offsets)).astype(jnp.bfloat16)
-            dq_ref[at, side] = (dot(key, dscores, TN) * SCALE).T.astype(jnp.bfloat16)
-            dv_acc[h] += dot(weights[block:], up)
+            chances = odds[:, at]
+            dscores = (chances * (dot(vs[h], up, NT) - stat_out[h, 1:2, at])).astype(jnp.bfloat16)
+            dq_ref[at, side] = (dot(ks[h], dscores, TN) * SCALE).T.astype(jnp.bfloat16)
+            dv_acc[h] += dot(odds[block:, at].astype(jnp.bfloat16), up)
             dk_acc[h] += dot(dscores[block:], query)
             return carry
 
-        lax.fori_loop(0, block // chunk, step, 0)
+        lax.fori_loop(0, steps, step, 0)
 
     def stat_copy(h):
         return pltpu.make_async_remote_copy(
@@ -193,10 +273,9 @@
         z_all(Q, h).wait_recv()
         z_all(U, h).wait_recv()
         stat_copy(h).wait_recv()
-        side = slice(h * HEAD_DIM, (h + 1) * HEAD_DIM)
 
         def step(c, carry):
-            at = pl.ds(pl.multiple_of(c * chunk, chunk), chunk)
+            at = chunk_at(c)
             there = pl.ds(pl.multiple_of(c * chunk + block, chunk), chunk)
             query, up = qs[h, there, :], us[h, there, :]
             key, value = ks[h, block:, :], vs[h, block:, :]
@@ -208,22 +287,52 @@
             dk_acc[h] += dot(dscores.astype(jnp.bfloat16), query)
             return carry
 
-        lax.fori_loop(0, block // chunk, step, 0)
+        lax.fori_loop(0, steps, step, 0)
+
+    for h in range(heads_here):
+        scores_of(h)
+        output_of(h)
+
+        @pl.when(has_before)
+        def _():
+            stat_copy(h).start()
+
+        grads_of(h)
+
+    for h in range(heads_here):
+
+        @pl.when(has_after)
+        def _():
+            cross(h)
+
+        side = slice(h * HEAD_DIM, (h + 1) * HEAD_DIM)
         dk_ref[:, side] = (dk_acc[h] * SCALE).astype(jnp.bfloat16)
         dv_ref[:, side] = dv_acc[h].astype(jnp.bfloat16)
 
     for h in range(heads_here):
-        main(h)
-        stat_copy(h).start()
-    for h in range(heads_here):
-        cross(h)
-
-    for h in range(heads_here):
-        stat_copy(h).wait_send()
         for a in (K, V, Q):
             x_sent(a, h).wait_send()
-        for a in (K, V, Q, U):
-            z_all(a, h).wait_send()
+
+        @pl.when(has_after)
+        def _():
+            for a in (K, V):
+                z_all(a, h).wait_send()
+
+        @pl.when(has_before)
+        def _():
+            stat_copy(h).wait_send()
+            for a in (Q, U):
+                z_all(a, h).wait_send()
+
+
+def store(*refs):
+    count = (len(refs) - 1) // 2
+    held, outs, sems = refs[:count], refs[count : 2 * count], refs[-1]
+    copies = [pltpu.make_async_copy(held[i], outs[i], sems.at[i]) for i in range(count)]
+    for copy in copies:
+        copy.start()
+    for copy in copies:
+        copy.wait()
 
 
 def on_device(queries, key_states, value_states, upstream, clip_lengths):
@@ -235,9 +344,10 @@
     hbm = pl.BlockSpec(memory_space=pl.ANY)
     vmem = pl.BlockSpec(memory_space=pltpu.VMEM)
     out = jax.ShapeDtypeStruct((block, wide), jnp.bfloat16)
-    return pl.pallas_call(
+    inside = pltpu.VMEM((block, wide), jnp.bfloat16)
+    results = pl.pallas_call(
         functools.partial(kernel, heads_here, blocks, chunk),
-        out_shape=(out,) * 4,
+        out_shape=(inside,) * 4,
         in_specs=[hbm] * 4 + [pl.BlockSpec(memory_space=pltpu.SMEM)],
         out_specs=(vmem,) * 4,
         scratch_shapes=[
@@ -258,9 +368,18 @@
             pltpu.SemaphoreType.DMA((4, heads_here)),
             pltpu.SemaphoreType.DMA((heads_here,)),
             pltpu.SemaphoreType.DMA((heads_here,)),
+            pltpu.SemaphoreType.REGULAR,
+            pltpu.VMEM((2 * block, block), jnp.float32),
         ],
         compiler_params=pltpu.CompilerParams(collective_id=0, has_side_effects=True),
     )(queries, key_states, value_states, upstream, clip_lengths)
+    return pl.pallas_call(
+        store,
+        out_shape=(out,) * 4,
+        in_specs=[vmem] * 4,
+        out_specs=(hbm,) * 4,
+        scratch_shapes=[pltpu.SemaphoreType.DMA((4,))],
+    )(*[pltpu.with_memory_space_constraint(r, pltpu.VMEM) for r in results])
 
 
 def solution(mesh):

time: 49.6 us -> 42.8 us (0.86)
  the two profiles are of different devices: /device:TPU:16 before, /device:TPU:57 now
where the time goes in v2:
time: 42.8 us; the launch traced here: 42.6 us
  Pallas kernels  42 us (98%)
  between operations  0.64 us (1%)
    pallas_call x1, Pallas kernels, on_device(): pl.pallas_call(functools.partial(kernel, heads_here, blocks, chunk), out_...  41 us
    pallas_call x1, Pallas kernels, on_device(): pl.pallas_call(store, out_shape=(out,) * 4, in_specs=[vmem] * 4, out_spec...  1 us

profile of v2, /device:TPU:57, one launch (start us, length us, event | category | flops | bytes accessed | tf_op | source)
XLA Modules:
  0.0 42.6 jit_solution(12641890702539475096)
XLA Ops:
  0.6 41.0 %shard_map.84 = (bf16[512,256]{1,0:T(8,128)(2,1)S(1)}, bf16[512,256]{1,0:T(8,128)(2,1)S(1)}, bf16[512,256]{1,0:T(8,128)(2,1)S(1)}, bf16[512,256]{1,0:T(8,128)(2,1)S(1)}) custom-call(bf16[64,2048]{1,0:T(8,128)(2,1)} %q_hbm.1, bf16[64,2048]{1,0:T(8,128)(2,1)} %k_hbm.1, bf16[64,2048]{1,0:T(8,128)(2,1)} %v_hbm.1, bf16[512,256]{1,0:T(8,128)(2,1)} %u_hbm.1, s32[32]{0:T(128)} %lengths.1), custom_call_target="tpu_custom_call" | custom-call | tf_op jit(solution)/shard_map/pallas_call | solution.py:348
  41.6 1.0 %shard_map.85 = (bf16[512,256]{1,0:T(8,128)(2,1)}, bf16[512,256]{1,0:T(8,128)(2,1)}, bf16[512,256]{1,0:T(8,128)(2,1)}, bf16[512,256]{1,0:T(8,128)(2,1)}) custom-call(bf16[512,256]{1,0:T(8,128)(2,1)S(1)} %get-tuple-element.8.refs_0_, bf16[512,256]{1,0:T(8,128)(2,1)S(1)} %get-tuple-element.9.refs_1_, bf16[512,256]{1,0:T(8,128)(2,1)S(1)} %get-tuple-element.10.refs_2_, ...), custom_call_target="tpu_custom_call" | custom-call | tf_op jit(solution)/shard_map/pallas_call | solution.py:376

commit v3 on v2

--- a/solution.py
+++ b/solution.py
@@ -28,7 +28,7 @@
     q_hbm, k_hbm, v_hbm, u_hbm, lengths,
     att_ref, dq_ref, dk_ref, dv_ref,
     ks, vs, qs, us, kid, qid, stat_out, stat_in, dk_acc, dv_acc,
-    own_sem, sx, rx, sz, rz, ss, rs, ready, odds,
+    own_sem, sx, rx, sz, rz, ss, rs, ready, led, rr, odds,
 ):
     part, blk, me = lax.axis_index("dp"), lax.axis_index("blk"), lax.axis_index("head")
     group = lax.axis_size("head")
@@ -61,11 +61,14 @@
         return (part, after, me) if a in (K, V) else (part, before, me)
 
     def x_copy(a, h, dx, dc, owner, target):
+        return x_at(a, h, dx * 2 + dc, owner, target)
+
+    def x_at(a, h, slot, owner, target):
         return pltpu.make_async_remote_copy(
             src_ref=inputs[a].at[:, columns(target, h)],
             dst_ref=held[a].at[h, place(owner, own_half(a)), :],
             send_sem=sx.at[a, h],
-            recv_sem=rx.at[a, h, dx * 2 + dc],
+            recv_sem=rx.at[a, h, slot],
             device_id=(part, blk, target),
             device_id_type=MESH,
         )
@@ -104,47 +107,34 @@
                 held[a].at[h, place(me, own_half(a)), :], own_sem.at[a, h]))
         own.append(pltpu.make_async_copy(
             u_hbm.at[:, h * HEAD_DIM : (h + 1) * HEAD_DIM], us.at[h, 0:block, :], own_sem.at[U, h]))
+    has_after, has_before = blk < blocks - 1, blk > 0
+    half, last = blocks // 2, blocks - 1
+    late_before = blk == half
+    leads_half, relays = blk == half - 1, blk == last
+    late_group = (part == 0) & (blk == 0)
+    leader, member = late_group & (me == 0), late_group & (me > 0)
+
     barrier = pltpu.get_barrier_semaphore()
-    for dx, dc in PARTNERS:
-        pl.semaphore_signal(barrier, inc=1, device_id=(part, blk, to(dx, dc)), device_id_type=MESH)
-
-    @pl.when(blk > 0)
+
+    @pl.when(jnp.logical_not(leader))
+    def _():
+        for dx, dc in PARTNERS:
+            pl.semaphore_signal(barrier, inc=1, device_id=(part, blk, to(dx, dc)), device_id_type=MESH)
+
+    @pl.when(has_before)
     def _():
         pl.semaphore_signal(barrier, inc=1, device_id=(part, before, me), device_id_type=MESH)
+
+    @pl.when(late_before)
+    def _():
+        pl.semaphore_signal(barrier, inc=1, device_id=(part, last, me), device_id_type=MESH)
+
+    @pl.when(relays)
+    def _():
+        pl.semaphore_signal(barrier, inc=1, device_id=(part, half - 1, me), device_id_type=MESH)
 
     for copy in own:
         copy.start()
-
-    spread = 3 * block
-    positions = (blk - 1) * block + lax.broadcasted_iota(jnp.int32, (1, spread), 1)
-    counted = jnp.zeros((1, spread), jnp.int32)
-    end = jnp.int32(0)
-    for c in range(lengths.shape[0]):
-        end = end + lengths[c]
-        counted = counted + jnp.where(positions >= end, 1, 0)
-    inside = (positions >= 0) & (positions < blocks * block)
-    ids = jnp.where(inside, counted, -1)
-    qid[...] = jnp.broadcast_to(ids[:, block:], qid.shape)
-    for c in range(2 * block // HEAD_DIM):
-        one = jnp.broadcast_to(ids[:, c * HEAD_DIM : (c + 1) * HEAD_DIM], (HEAD_DIM, HEAD_DIM))
-        turned = one.T
-        for n in range(chunk // HEAD_DIM):
-            kid[c * HEAD_DIM : (c + 1) * HEAD_DIM, n * HEAD_DIM : (n + 1) * HEAD_DIM] = turned
-
-    @pl.when(blk == 0)
-    def _():
-        for h in range(heads_here):
-            ks[h, 0:block, :] = jnp.zeros((block, HEAD_DIM), jnp.bfloat16)
-            vs[h, 0:block, :] = jnp.zeros((block, HEAD_DIM), jnp.bfloat16)
-
-    pl.semaphore_wait(barrier, len(PARTNERS) + 1 - blk // (blocks - 1))
-
-    has_after, has_before = blk < blocks - 1, blk > 0
-    late_before = blk == blocks // 2
-
-    @pl.when(has_after)
-    def _():
-        pl.semaphore_signal(ready, inc=1, device_id=(part, after, me), device_id_type=MESH)
 
     def back_up(h):
         pltpu.make_async_remote_copy(
@@ -156,51 +146,167 @@
             device_id_type=MESH,
         ).start()
 
-    def own_on(a, h):
-        z_copy(a, h, me, inputs[a].at[:, columns(me, h)]).start()
-
-    def on(a, h, owner):
-        z_copy(a, h, owner, held[a].at[h, place(owner, own_half(a)), :]).start()
-
-    for h in range(heads_here):
-        for a in (K, V):
+    def relay_in(h, owner, src):
+        return pltpu.make_async_remote_copy(
+            src_ref=src,
+            dst_ref=us.at[h, place(owner, 1), :],
+            send_sem=sz.at[V, h],
+            recv_sem=rr.at[h, owner],
+            device_id=(part, last, me),
+            device_id_type=MESH,
+        )
+
+    def relay_out(h, owner):
+        return pltpu.make_async_remote_copy(
+            src_ref=us.at[h, place(owner, 1), :],
+            dst_ref=vs.at[h, place(owner, 0), :],
+            send_sem=sz.at[V, h],
+            recv_sem=rz.at[V, h],
+            device_id=(part, half, me),
+            device_id_type=MESH,
+        )
+
+    def at_home(a, h, owner):
+        return held[a].at[h, place(owner, own_half(a)), :]
+
+    def own_rows(a, h):
+        return inputs[a].at[:, columns(me, h)]
+
+    order = [(a, h) for h in range(heads_here) for a in (K, V)] + [(Q, h) for h in range(heads_here)]
+
+    def prepare():
+        spread = 3 * block
+        positions = (blk - 1) * block + lax.broadcasted_iota(jnp.int32, (1, spread), 1)
+        counted = jnp.zeros((1, spread), jnp.int32)
+        end = jnp.int32(0)
+        for c in range(lengths.shape[0]):
+            end = end + lengths[c]
+            counted = counted + jnp.where(positions >= end, 1, 0)
+        inside = (positions >= 0) & (positions < blocks * block)
+        ids = jnp.where(inside, counted, -1)
+        qid[...] = jnp.broadcast_to(ids[:, block:], qid.shape)
+        for c in range(2 * block // HEAD_DIM):
+            one = jnp.broadcast_to(ids[:, c * HEAD_DIM : (c + 1) * HEAD_DIM], (HEAD_DIM, HEAD_DIM))
+            turned = one.T
+            for n in range(chunk // HEAD_DIM):
+                kid[c * HEAD_DIM : (c + 1) * HEAD_DIM, n * HEAD_DIM : (n + 1) * HEAD_DIM] = turned
+
+        @pl.when(blk == 0)
+        def _():
+            for h in range(heads_here):
+                ks[h, 0:block, :] = jnp.zeros((block, HEAD_DIM), jnp.bfloat16)
+                vs[h, 0:block, :] = jnp.zeros((block, HEAD_DIM), jnp.bfloat16)
+
+        for h in range(heads_here):
+            dk_acc[h] = jnp.zeros_like(dk_acc[h])
+            dv_acc[h] = jnp.zeros_like(dv_acc[h])
+
+    def traffic(peers, to_after, to_before, aside=False, relay=False, late=False, wait_leader=False):
+        pl.semaphore_wait(barrier, peers)
+
+        if to_after and not to_before and not wait_leader:
+
+            @pl.when(leader)
+            def _():
+                for dx, dc in PARTNERS:
+                    pl.semaphore_signal(led, inc=1, device_id=(part, blk, to(dx, dc)), device_id_type=MESH)
+
+        if to_after:
+            pl.semaphore_signal(ready, inc=1, device_id=(part, after, me), device_id_type=MESH)
+
+        def pass_on(a, h, owner, src):
+            if a == Q:
+                if to_before and not late:
+                    z_copy(a, h, owner, src).start()
+            elif to_after:
+                if aside and a == V:
+                    relay_in(h, owner, src).start()
+                else:
+                    z_copy(a, h, owner, src).start()
+
+        def start(a, h, dx, dc):
+            if wait_leader:
+
+                @pl.when(to(dx, dc) != 0)
+                def _():
+                    x_copy(a, h, dx, dc, me, to(dx, dc)).start()
+            else:
+                x_copy(a, h, dx, dc, me, to(dx, dc)).start()
+
+        def take(a, h, dx, dc):
+            owner = source(dx, dc)
+
+            def now():
+                x_copy(a, h, dx, dc, owner, me).wait_recv()
+                pass_on(a, h, owner, at_home(a, h, owner))
+
+            if wait_leader:
+                pl.when(owner != 0)(now)
+            else:
+                now()
+
+        def send_back():
+            pl.semaphore_wait(ready, 1)
+            for h in range(heads_here):
+                back_up(h)
+                z_copy(Q, h, me, own_rows(Q, h)).start()
+
+        def send(a, h):
+            if a != Q:
+                pass_on(a, h, me, own_rows(a, h))
             for dx, dc in PARTNERS:
-                x_copy(a, h, dx, dc, me, to(dx, dc)).start()
-
-            @pl.when(has_after)
-            def _():
-                own_on(a, h)
-
-        for dx, dc in PARTNERS:
-            x_copy(Q, h, dx, dc, me, to(dx, dc)).start()
-
-    early_back = has_before & jnp.logical_not(late_before)
-
-    @pl.when(early_back)
-    def _():
-        pl.semaphore_wait(ready, 1)
-        for h in range(heads_here):
-            back_up(h)
-            own_on(Q, h)
-
-    for h in range(heads_here):
-        for a in (K, V, Q):
+                start(a, h, dx, dc)
+
+        for a, h in order:
+            send(a, h)
+        if to_before and not late:
+            send_back()
+        prepare()
+        for a, h in order:
             for dx, dc in PARTNERS:
-                owner = source(dx, dc)
-                x_copy(a, h, dx, dc, owner, me).wait_recv()
-
-                @pl.when(early_back if a == Q else has_after)
-                def _():
-                    on(a, h, owner)
+                take(a, h, dx, dc)
+            if relay and a == V:
+                for owner in range(group):
+                    relay_in(h, owner, us.at[h, place(owner, 1), :]).wait_recv()
+                    relay_out(h, owner).start()
+        if wait_leader:
+            pl.semaphore_wait(led, 1)
+            back = lax.rem(chips - chip, chips) * 2 + core
+            for a, h in order:
+                x_at(a, h, back, me, 0).start()
+            for a, h in order:
+                x_at(a, h, me, 0, me).wait_recv()
+                pass_on(a, h, 0, at_home(a, h, 0))
+        if late:
+            send_back()
+            for h in range(heads_here):
+                for dx, dc in PARTNERS:
+                    owner = source(dx, dc)
+                    z_copy(Q, h, owner, at_home(Q, h, owner)).start()
+
+    @pl.when(has_before & has_after & (blk != half - 1) & (blk != half))
+    def _():
+        traffic(len(PARTNERS) + 1, True, True)
+
+    @pl.when((blk == 0) & jnp.logical_not(member))
+    def _():
+        traffic(len(PARTNERS) + 1, True, False)
+
+    @pl.when(member)
+    def _():
+        traffic(len(PARTNERS), True, False, wait_leader=True)
+
+    @pl.when(leads_half)
+    def _():
+        traffic(len(PARTNERS) + 2, True, True, aside=True)
 
     @pl.when(late_before)
     def _():
-        pl.semaphore_wait(ready, 1)
-        for h in range(heads_here):
-            back_up(h)
-            own_on(Q, h)
-            for dx, dc in PARTNERS:
-                on(Q, h, source(dx, dc))
+        traffic(len(PARTNERS) + 1, True, True, late=True)
+
+    @pl.when(relays)
+    def _():
+        traffic(len(PARTNERS) + 1, False, True, relay=True)
 
     for copy in own:
         copy.wait()
@@ -248,8 +354,6 @@
 
     def grads_of(h):
         side = slice(h * HEAD_DIM, (h + 1) * HEAD_DIM)
-        dk_acc[h] = jnp.zeros_like(dk_acc[h])
-        dv_acc[h] = jnp.zeros_like(dv_acc[h])
 
         def step(c, carry):
             at = chunk_at(c)
@@ -289,6 +393,14 @@
 
         lax.fori_loop(0, steps, step, 0)
 
+    cross_first = late_before | ((part == 0) & (blk == 1))
+    cross_later = has_after & jnp.logical_not(cross_first)
+
+    @pl.when(cross_first)
+    def _():
+        for h in range(heads_here):
+            cross(h)
+
     for h in range(heads_here):
         scores_of(h)
         output_of(h)
@@ -299,12 +411,12 @@
 
         grads_of(h)
 
+    @pl.when(cross_later)
+    def _():
+        for h in range(heads_here):
+            cross(h)
+
     for h in range(heads_here):
-
-        @pl.when(has_after)
-        def _():
-            cross(h)
-
         side = slice(h * HEAD_DIM, (h + 1) * HEAD_DIM)
         dk_ref[:, side] = (dk_acc[h] * SCALE).astype(jnp.bfloat16)
         dv_ref[:, side] = dv_acc[h].astype(jnp.bfloat16)
@@ -315,8 +427,11 @@
 
         @pl.when(has_after)
         def _():
-            for a in (K, V):
-                z_all(a, h).wait_send()
+            z_all(K, h).wait_send()
+
+        @pl.when(has_after | relays)
+        def _():
+            z_all(V, h).wait_send()
 
         @pl.when(has_before)
         def _():
@@ -338,7 +453,7 @@
 def on_device(queries, key_states, value_states, upstream, clip_lengths):
     block, wide = upstream.shape
     heads_here = wide // HEAD_DIM
-    chunk = 256
+    chunk = 512
     group = lax.axis_size("head")
     blocks = lax.axis_size("blk")
     hbm = pl.BlockSpec(memory_space=pl.ANY)
@@ -369,6 +484,8 @@
             pltpu.SemaphoreType.DMA((heads_here,)),
             pltpu.SemaphoreType.DMA((heads_here,)),
             pltpu.SemaphoreType.REGULAR,
+            pltpu.SemaphoreType.REGULAR,
+            pltpu.SemaphoreType.DMA((heads_here, group)),
             pltpu.VMEM((2 * block, block), jnp.float32),
         ],
         compiler_params=pltpu.CompilerParams(collective_id=0, has_side_effects=True),

time: 42.8 us -> 40.4 us (0.944)
  Pallas kernels: 42 us -> 39.1 us
    pallas_call x1, Pallas kernels: 41 us -> 38.1 us  [on_device(): pl.pallas_call(functools.partial(kernel, heads_here, blocks, chunk), out_...]
where the time goes in v3:
time: 40.4 us; the launch traced here: 39.9 us
  Pallas kernels  39.1 us (97%)
  between operations  0.8 us (2%)
    pallas_call x1, Pallas kernels, on_device(): pl.pallas_call(functools.partial(kernel, heads_here, blocks, chunk), out_...  38.1 us
    pallas_call x1, Pallas kernels, on_device(): pl.pallas_call(store, out_shape=(out,) * 4, in_specs=[vmem] * 4, out_spec...  1 us

profile of v3, /device:TPU:57, one launch (start us, length us, event | category | flops | bytes accessed | tf_op | source)
XLA Modules:
  0.0 39.9 jit_solution(10660788233256024766)
XLA Ops:
  0.6 38.1 %shard_map.84 = (bf16[512,256]{1,0:T(8,128)(2,1)S(1)}, bf16[512,256]{1,0:T(8,128)(2,1)S(1)}, bf16[512,256]{1,0:T(8,128)(2,1)S(1)}, bf16[512,256]{1,0:T(8,128)(2,1)S(1)}) custom-call(bf16[64,2048]{1,0:T(8,128)(2,1)} %q_hbm.1, bf16[64,2048]{1,0:T(8,128)(2,1)} %k_hbm.1, bf16[64,2048]{1,0:T(8,128)(2,1)} %v_hbm.1, bf16[512,256]{1,0:T(8,128)(2,1)} %u_hbm.1, s32[32]{0:T(128)} %lengths.1), custom_call_target="tpu_custom_call" | custom-call | tf_op jit(solution)/shard_map/pallas_call | solution.py:463
  38.7 1.0 %shard_map.85 = (bf16[512,256]{1,0:T(8,128)(2,1)}, bf16[512,256]{1,0:T(8,128)(2,1)}, bf16[512,256]{1,0:T(8,128)(2,1)}, bf16[512,256]{1,0:T(8,128)(2,1)}) custom-call(bf16[512,256]{1,0:T(8,128)(2,1)S(1)} %get-tuple-element.8.refs_0_, bf16[512,256]{1,0:T(8,128)(2,1)S(1)} %get-tuple-element.9.refs_1_, bf16[512,256]{1,0:T(8,128)(2,1)S(1)} %get-tuple-element.10.refs_2_, ...), custom_call_target="tpu_custom_call" | custom-call | tf_op jit(solution)/shard_map/pallas_call | solution.py:493

commit v4 on v3

--- a/solution.py
+++ b/solution.py
@@ -266,7 +266,7 @@
             for dx, dc in PARTNERS:
                 take(a, h, dx, dc)
             if relay and a == V:
-                for owner in range(group):
+                for owner in [me] + [source(dx, dc) for dx, dc in PARTNERS]:
                     relay_in(h, owner, us.at[h, place(owner, 1), :]).wait_recv()
                     relay_out(h, owner).start()
         if wait_leader:
@@ -443,7 +443,14 @@
 def store(*refs):
     count = (len(refs) - 1) // 2
     held, outs, sems = refs[:count], refs[count : 2 * count], refs[-1]
-    copies = [pltpu.make_async_copy(held[i], outs[i], sems.at[i]) for i in range(count)]
+    rows = held[0].shape[0] // 2
+    copies = [
+        pltpu.make_async_copy(
+            held[i].at[n * rows : (n + 1) * rows], outs[i].at[n * rows : (n + 1) * rows], sems.at[i, n]
+        )
+        for i in range(count)
+        for n in range(2)
+    ]
     for copy in copies:
         copy.start()
     for copy in copies:
@@ -495,7 +502,7 @@
         out_shape=(out,) * 4,
         in_specs=[vmem] * 4,
         out_specs=(hbm,) * 4,
-        scratch_shapes=[pltpu.SemaphoreType.DMA((4,))],
+        scratch_shapes=[pltpu.SemaphoreType.DMA((4, 2))],
     )(*[pltpu.with_memory_space_constraint(r, pltpu.VMEM) for r in results])
 
 

time: 40.4 us -> 39.9 us (0.988)
  Pallas kernels: 39.1 us -> 38.3 us
    pallas_call x1, Pallas kernels: 38.1 us -> 37.2 us  [on_device(): pl.pallas_call(functools.partial(kernel, heads_here, blocks, chunk), out_...]
where the time goes in v4:
time: 39.9 us; the launch traced here: 39.1 us
  Pallas kernels  38.3 us (96%)
  between operations  0.8 us (2%)
    pallas_call x1, Pallas kernels, on_device(): pl.pallas_call(functools.partial(kernel, heads_here, blocks, chunk), out_...  37.2 us
    pallas_call x1, Pallas kernels, on_device(): pl.pallas_call(store, out_shape=(out,) * 4, in_specs=[vmem] * 4, out_spec...  1.03 us

profile of v4, /device:TPU:57, one launch (start us, length us, event | category | flops | bytes accessed | tf_op | source)
XLA Modules:
  0.0 39.1 jit_solution(5828021972417872130)
XLA Ops:
  0.6 37.2 %shard_map.84 = (bf16[512,256]{1,0:T(8,128)(2,1)S(1)}, bf16[512,256]{1,0:T(8,128)(2,1)S(1)}, bf16[512,256]{1,0:T(8,128)(2,1)S(1)}, bf16[512,256]{1,0:T(8,128)(2,1)S(1)}) custom-call(bf16[64,2048]{1,0:T(8,128)(2,1)} %q_hbm.1, bf16[64,2048]{1,0:T(8,128)(2,1)} %k_hbm.1, bf16[64,2048]{1,0:T(8,128)(2,1)} %v_hbm.1, bf16[512,256]{1,0:T(8,128)(2,1)} %u_hbm.1, s32[32]{0:T(128)} %lengths.1), custom_call_target="tpu_custom_call" | custom-call | tf_op jit(solution)/shard_map/pallas_call | solution.py:470
  37.9 1.0 %shard_map.85 = (bf16[512,256]{1,0:T(8,128)(2,1)}, bf16[512,256]{1,0:T(8,128)(2,1)}, bf16[512,256]{1,0:T(8,128)(2,1)}, bf16[512,256]{1,0:T(8,128)(2,1)}) custom-call(bf16[512,256]{1,0:T(8,128)(2,1)S(1)} %get-tuple-element.8.refs_0_, bf16[512,256]{1,0:T(8,128)(2,1)S(1)} %get-tuple-element.9.refs_1_, bf16[512,256]{1,0:T(8,128)(2,1)S(1)} %get-tuple-element.10.refs_2_, ...), custom_call_target="tpu_custom_call" | custom-call | tf_op jit(solution)/shard_map/pallas_call | solution.py:500
